TPU v7x, 128 devices: a whole 4x4x4 slice. The times are simulated.
128 devices in a mesh: pair: 2 (over x_hi), gx: 8 (over y, x_lo), gy: 8 (over z, core).
Axes of the slice: x: 4 (x_hi: 2, x_lo: 2; x = x_hi * 2 + x_lo), y: 4, z: 4, core: 2. Of those that a mesh axis runs over, the one named last changes fastest.
Arguments:
- sound_speed_sq: float32 [64, 64, 1024], P('gx', 'gy'), may hold values from 0.5 to 2
- wind_profile: float32 [3, 1024], replicated, may hold values from -0.6 to 0.6
- forward_field: bfloat16 [4, 4, 64, 64, 1024], P(None, None, 'gx', 'gy'), may hold values from -6 to 6
- adjoint_state: float32 [2, 4, 64, 64, 1024], P('pair', None, 'gx', 'gy'), may hold values from -0.3125 to 0.3125
- pair_counts: int32 [2], P('pair'), may hold values from 64 to 256, as said below
- source_cells: int32 [512, 3], P('pair'), may hold values from 0 to 1023, as said below
- receiver_cells: int32 [512, 3], P('pair'), may hold values from 0 to 1023, as said below
- residuals: float32 [512, 4], P('pair'), may hold values from -16 to 16
Outputs:
- kernels: float32 [4, 64, 64, 1024], P(None, 'gx', 'gy', 'pair')
- final_state: float32 [2, 4, 64, 64, 1024], P('pair', None, 'gx', 'gy')
Inputs may be any that keep to these rules, and one draw needn't show every extreme that they name: `pair_counts`: one group in every draw has exactly 256 live pairs. `source_cells`: columns are the cell along the first, second and third dimension, each within the grid. `receiver_cells`: columns are the cell along the first, second and third dimension, each within the grid; several pairs may share a cell.
All inputs are finite; a program needn't handle non-finite values.
Results may differ from a plain program's by a relative error of at most 0.00115.
Values may be sent and summed in bfloat16 or wider, within the bound.
A program may use at most 128 MiB of HBM per device.

v0:
```python
import jax
import jax.numpy as jnp
from jax import lax
from jax.sharding import PartitionSpec as P

step_length = 0.25


def neighbours(shard, axis, dim):
    size, length = (lax.axis_size(axis), shard.shape[dim])
    up = [(i, i + 1) for i in range(size - 1)]
    down = [(i + 1, i) for i in range(size - 1)]
    last = lax.slice_in_dim(shard, length - 1, length, axis=dim)
    first = lax.slice_in_dim(shard, 0, 1, axis=dim)
    before = lax.ppermute(last, axis, up)
    after = lax.ppermute(first, axis, down)
    return (before, after)


def halos(shard, dim_x, dim_y):
    return (neighbours(shard, "gx", dim_x), neighbours(shard, "gy", dim_y))


def central(field, rims):
    (west, east), (south, north) = rims
    dims = field.ndim
    x_hi = jnp.concatenate(
        [lax.slice_in_dim(field, 1, field.shape[-3], axis=dims - 3), east], axis=dims - 3
    )
    x_lo = jnp.concatenate(
        [west, lax.slice_in_dim(field, 0, field.shape[-3] - 1, axis=dims - 3)], axis=dims - 3
    )
    y_hi = jnp.concatenate(
        [lax.slice_in_dim(field, 1, field.shape[-2], axis=dims - 2), north], axis=dims - 2
    )
    y_lo = jnp.concatenate(
        [south, lax.slice_in_dim(field, 0, field.shape[-2] - 1, axis=dims - 2)], axis=dims - 2
    )
    east_diff = (x_hi - x_lo) * 0.5
    north_diff = (y_hi - y_lo) * 0.5
    vertical = jnp.pad(field, [(0, 0)] * (dims - 1) + [(1, 1)])
    up_diff = (vertical[..., 2:] - vertical[..., :-2]) * 0.5
    return (east_diff, north_diff, up_diff)


def local_cells(cells, width_x, width_y):
    local_x = cells[:, 0] - lax.axis_index("gx") * width_x
    local_y = cells[:, 1] - lax.axis_index("gy") * width_y
    inside = (local_x >= 0) & (local_x < width_x) & (local_y >= 0) & (local_y < width_y)
    return (
        jnp.clip(local_x, 0, width_x - 1),
        jnp.clip(local_y, 0, width_y - 1),
        cells[:, 2],
        inside.astype(jnp.float32),
    )


def shards(
    sound_speed_sq,
    wind_profile,
    forward_field,
    adjoint_state,
    pair_counts,
    source_cells,
    receiver_cells,
    residuals,
):
    steps_total = forward_field.shape[0]
    width_x, width_y, depth = sound_speed_sq.shape
    slots = residuals.shape[0]
    east_wind = wind_profile[0]
    north_wind = wind_profile[1]
    vertical_wind = wind_profile[2]
    live = (jnp.arange(slots, dtype=jnp.int32) < pair_counts[0]).astype(jnp.float32)
    sx, sy, sz, src_inside = local_cells(source_cells, width_x, width_y)
    rx, ry, rz, rcv_inside = local_cells(receiver_cells, width_x, width_y)
    local_samples = (
        jnp.stack([forward_field[t, 0][sx, sy, sz] for t in range(steps_total)]).astype(jnp.float32)
        * src_inside[None, :]
    )
    me = lax.axis_index("pair")
    slot = jnp.zeros((lax.axis_size("pair"),) + local_samples.shape, jnp.float32)
    samples = lax.psum(slot.at[me].set(local_samples), ("pair", "gx", "gy"))[me]
    forward_rims = halos(forward_field, 2, 3)
    rcv_flat = (rx * width_y + ry) * depth + rz
    state = adjoint_state[0]
    kernel_local = jnp.zeros((4, width_x, width_y, depth), jnp.float32)
    for step in range(steps_total):
        snap = steps_total - 1 - step
        amplitude = residuals[:, snap] * samples[snap] * live * rcv_inside
        injected = (
            jnp.zeros((width_x * width_y * depth,), jnp.float32)
            .at[rcv_flat]
            .add(amplitude)
            .reshape(width_x, width_y, depth)
        )
        east_diff, north_diff, up_diff = central(state, halos(state, 1, 2))
        pressure = state[0]
        velocity = state[1:]
        divergence = east_diff[1] + north_diff[2] + up_diff[3]
        p_new = (
            pressure
            + step_length
            * (
                sound_speed_sq * divergence
                + east_wind * east_diff[0]
                + north_wind * north_diff[0]
                + vertical_wind * up_diff[0]
            )
            + injected
        )
        p_east, p_north, p_up = central(p_new, halos(p_new, 0, 1))
        gradient = jnp.stack([p_east, p_north, p_up])
        a_new = velocity + step_length * (
            gradient
            + east_wind * east_diff[1:]
            + north_wind * north_diff[1:]
            + vertical_wind * up_diff[1:]
        )
        forward = forward_field[snap].astype(jnp.float32)
        rims = tuple(
            (tuple((side[snap].astype(jnp.float32) for side in pair)) for pair in forward_rims)
        )
        f_east, f_north, f_up = central(forward, rims)
        pieces = [p_new * (f_east[1] + f_north[2] + f_up[3])]
        for along in (f_east, f_north, f_up):
            pieces.append(
                p_new * along[0] + a_new[0] * along[1] + a_new[1] * along[2] + a_new[2] * along[3]
            )
        increment = jnp.stack(pieces)
        kernel_local = kernel_local + increment
        state = jnp.concatenate([p_new[None], a_new], axis=0)
    kernels = lax.psum_scatter(kernel_local, "pair", scatter_dimension=3, tiled=True)
    return (kernels, state[None])


def solution(mesh):
    in_specs = (
        P("gx", "gy", None),
        P(),
        P(None, None, "gx", "gy", None),
        P("pair", None, "gx", "gy", None),
        P("pair"),
        P("pair", None),
        P("pair", None),
        P("pair", None),
    )
    out_specs = (P(None, "gx", "gy", "pair"), P("pair", None, "gx", "gy", None))
    return jax.shard_map(shards, mesh=mesh, in_specs=in_specs, out_specs=out_specs, check_vma=False)
```

profile of v0, /device:TPU:1, one launch (start us, length us, event | category | flops | bytes accessed | tf_op | source)
XLA Modules:
  0.0 314.3 jit_solution(12173777314110619622)
XLA Ops:
  7.2 2.1 slice_bitcast_fusion.32
  9.3 1.4 collective-permute-start.4
  10.7 5.3 %collective-permute-start.5 = (bf16[4,4,1,8,1024]{4,3,1,2,0:T(8,128)(2,1)}, bf16[4,4,1,8,1024]{4,3,1,2,0:T(8,128)(2,1)}, u32[]{:S(2)}, u32[]{:S(2)}) collective-permute-start(bf16[4,4,1,8,1024]{4,3,1,2,0:T(8,128)(2,1)} %get-tuple-element.30), channel_id=1, source_target_pairs={{0,8},{8,16},{16,24},{24,32},{32,40},{40,48},{48,56},{1,9},{9,17},... | collective-permute-start | bytes 786440 | tf_op jit(solution)/shard_map/ppermute | solution.py:15
  16.0 4.4 %fusion.266 = (bf16[4,4,8,1,1024]{4,3,2,1,0:T(2,128)(2,1)}, bf16[4,4,8,1,1024]{4,3,2,1,0:T(2,128)(2,1)}) fusion(bf16[4,4,8,8,1024]{4,3,2,1,0:T(8,128)(2,1)} %param.12), kind=kLoop, calls=%fused_computation.506 | loop fusion | bytes 1048576 | tf_op jit(solution)/shard_map/slice | solution.py:13
  20.4 3.3 %collective-permute-start.6 = (bf16[4,4,8,1,1024]{4,3,2,1,0:T(2,128)(2,1)}, bf16[4,4,8,1,1024]{4,3,2,1,0:T(2,128)(2,1)}, u32[]{:S(2)}, u32[]{:S(2)}) collective-permute-start(bf16[4,4,8,1,1024]{4,3,2,1,0:T(2,128)(2,1)} %get-tuple-element.33), channel_id=1, source_target_pairs={{1,0},{2,1},{3,2},{4,3},{5,4},{6,5},{7,6},{9,8},{10,9},{11,10},{12... | collective-permute-start | bytes 786440 | tf_op jit(solution)/shard_map/ppermute | solution.py:16
  24.6 1.9 collective-permute-start.2
  26.5 3.6 %collective-permute-start.3 = (f32[4,8,1,1024]{3,2,1,0:T(1,128)}, f32[4,8,1,1024]{3,2,1,0:T(1,128)}, u32[]{:S(2)}, u32[]{:S(2)}) collective-permute-start(f32[4,8,1,1024]{3,2,1,0:T(1,128)} %get-tuple-element.82), channel_id=1, source_target_pairs={{0,1},{1,2},{2,3},{3,4},{4,5},{5,6},{6,7},{8,9},{9,10},{10,11},{11... | collective-permute-start | bytes 393224 | tf_op jit(solution)/shard_map/ppermute | solution.py:15
  30.6 2.5 fusion.1
  33.1 2.0 fusion.271
  35.0 2.2 fusion.272
  37.3 1.8 slice_bitcast_fusion.53
  39.1 1.6 fusion.276
  41.4 1.5 fusion.274
  42.9 1.6 fusion.7
  44.5 1.6 fusion.11
  46.1 2.0 fusion.267
  48.1 2.2 fusion.268
  50.3 2.9 gather_fusion.3
  53.2 2.8 gather_fusion.2
  56.1 2.8 gather_fusion.1
  58.9 2.8 gather_fusion
  63.2 66.1 %psum.7 = f32[2,4,256]{2,1,0:T(4,128)S(1)} all-reduce(f32[2,4,256]{2,1,0:T(4,128)S(1)} %select_dynamic-update-slice_fusion), channel_id=1, replica_groups=mesh['pair'=2,'gx'=8,'gy'=8] {'pair','gx','gy'}, use_global_device_ids=true, to_apply=%region_1.2 | all-reduce | flops 2048 | bytes 16384 | tf_op jit(solution)/shard_map/psum | solution.py:83
  130.0 2.2 scatter_custom_fusion
  132.3 2.0 scatter_custom_fusion.1
  134.4 2.0 scatter_custom_fusion.2
  136.5 2.0 scatter_custom_fusion.3
  139.3 1.3 collective-permute-start
  140.6 4.0 %collective-permute-start.1 = (f32[4,1,8,1024]{3,2,1,0:T(8,128)S(1)}, f32[4,1,8,1024]{3,2,1,0:T(8,128)S(1)}, u32[]{:S(2)}, u32[]{:S(2)}) collective-permute-start(f32[4,1,8,1024]{3,2,1,0:T(8,128)S(1)} %copy-done.30), channel_id=1, source_target_pairs={{0,8},{8,16},{16,24},{24,32},{32,40},{40,48},{48,56},{1,9},{9,17},... | collective-permute-start | bytes 393224 | tf_op jit(solution)/shard_map/ppermute | solution.py:15
  144.7 1.6 fusion.23
  146.3 3.2 %collective-permute-start.7 = (bf16[4,4,8,1,1024]{4,3,2,1,0:T(2,128)(2,1)S(1)}, bf16[4,4,8,1,1024]{4,3,2,1,0:T(2,128)(2,1)S(1)}, u32[]{:S(2)}, u32[]{:S(2)}) collective-permute-start(bf16[4,4,8,1,1024]{4,3,2,1,0:T(2,128)(2,1)S(1)} %copy-done.29), channel_id=1, source_target_pairs={{0,1},{1,2},{2,3},{3,4},{4,5},{5,6},{6,7},{8,9},{9,10},{10,11},{11... | collective-permute-start | bytes 786440 | tf_op jit(solution)/shard_map/ppermute | solution.py:15
  152.2 1.8 fusion.231
  153.9 1.7 collective-permute-done.7
  158.2 2.1 collective-permute-start.10
  160.3 4.4 %collective-permute-start.11 = (f32[8,1,1024]{2,1,0:T(1,128)S(1)}, f32[8,1,1024]{2,1,0:T(1,128)S(1)}, u32[]{:S(2)}, u32[]{:S(2)}) collective-permute-start(f32[8,1,1024]{2,1,0:T(1,128)S(1)} %get-tuple-element.134), channel_id=1, source_target_pairs={{0,1},{1,2},{2,3},{3,4},{4,5},{5,6},{6,7},{8,9},{9,10},{10,11},{11... | collective-permute-start | bytes 98312 | tf_op jit(solution)/shard_map/ppermute | solution.py:15
  172.9 1.3 collective-permute-start.8
  174.2 4.7 %collective-permute-start.9 = (f32[1,8,1024]{2,1,0:T(8,128)S(1)}, f32[1,8,1024]{2,1,0:T(8,128)S(1)}, u32[]{:S(2)}, u32[]{:S(2)}) collective-permute-start(f32[1,8,1024]{2,1,0:T(8,128)S(1)} %get-tuple-element.130), channel_id=1, source_target_pairs={{0,8},{8,16},{16,24},{24,32},{32,40},{40,48},{48,56},{1,9},{9,17},... | collective-permute-start | bytes 98312 | tf_op jit(solution)/shard_map/ppermute | solution.py:15
  181.5 2.1 collective-permute-start.14
  183.6 3.6 %collective-permute-start.15 = (f32[4,8,1,1024]{3,2,1,0:T(1,128)S(1)}, f32[4,8,1,1024]{3,2,1,0:T(1,128)S(1)}, u32[]{:S(2)}, u32[]{:S(2)}) collective-permute-start(f32[4,8,1,1024]{3,2,1,0:T(1,128)S(1)} %get-tuple-element.68), channel_id=1, source_target_pairs={{0,1},{1,2},{2,3},{3,4},{4,5},{5,6},{6,7},{8,9},{9,10},{10,11},{11... | collective-permute-start | bytes 393224 | tf_op jit(solution)/shard_map/ppermute | solution.py:15
  187.3 1.3 collective-permute-start.12
  188.6 4.9 %collective-permute-start.13 = (f32[4,1,8,1024]{3,2,1,0:T(8,128)S(1)}, f32[4,1,8,1024]{3,2,1,0:T(8,128)S(1)}, u32[]{:S(2)}, u32[]{:S(2)}) collective-permute-start(f32[4,1,8,1024]{3,2,1,0:T(8,128)S(1)} %get-tuple-element.64), channel_id=1, source_target_pairs={{0,8},{8,16},{16,24},{24,32},{32,40},{40,48},{48,56},{1,9},{9,17},... | collective-permute-start | bytes 393224 | tf_op jit(solution)/shard_map/ppermute | solution.py:15
  194.6 1.5 collective-permute-done.13
  197.7 1.9 collective-permute-start.18
  199.6 3.9 %collective-permute-start.19 = (f32[8,1,1024]{2,1,0:T(1,128)S(1)}, f32[8,1,1024]{2,1,0:T(1,128)S(1)}, u32[]{:S(2)}, u32[]{:S(2)}) collective-permute-start(f32[8,1,1024]{2,1,0:T(1,128)S(1)} %get-tuple-element.126), channel_id=1, source_target_pairs={{0,1},{1,2},{2,3},{3,4},{4,5},{5,6},{6,7},{8,9},{9,10},{10,11},{11... | collective-permute-start | bytes 98312 | tf_op jit(solution)/shard_map/ppermute | solution.py:15
  203.7 1.3 collective-permute-start.16
  205.0 5.0 %collective-permute-start.17 = (f32[1,8,1024]{2,1,0:T(8,128)S(1)}, f32[1,8,1024]{2,1,0:T(8,128)S(1)}, u32[]{:S(2)}, u32[]{:S(2)}) collective-permute-start(f32[1,8,1024]{2,1,0:T(8,128)S(1)} %get-tuple-element.122), channel_id=1, source_target_pairs={{0,8},{8,16},{16,24},{24,32},{32,40},{40,48},{48,56},{1,9},{9,17},... | collective-permute-start | bytes 98312 | tf_op jit(solution)/shard_map/ppermute | solution.py:15
  212.7 1.9 collective-permute-start.22
  214.6 3.6 %collective-permute-start.23 = (f32[4,8,1,1024]{3,2,1,0:T(1,128)S(1)}, f32[4,8,1,1024]{3,2,1,0:T(1,128)S(1)}, u32[]{:S(2)}, u32[]{:S(2)}) collective-permute-start(f32[4,8,1,1024]{3,2,1,0:T(1,128)S(1)} %get-tuple-element.54), channel_id=1, source_target_pairs={{0,1},{1,2},{2,3},{3,4},{4,5},{5,6},{6,7},{8,9},{9,10},{10,11},{11... | collective-permute-start | bytes 393224 | tf_op jit(solution)/shard_map/ppermute | solution.py:15
  218.3 1.3 collective-permute-start.20
  219.6 5.6 %collective-permute-start.21 = (f32[4,1,8,1024]{3,2,1,0:T(8,128)S(1)}, f32[4,1,8,1024]{3,2,1,0:T(8,128)S(1)}, u32[]{:S(2)}, u32[]{:S(2)}) collective-permute-start(f32[4,1,8,1024]{3,2,1,0:T(8,128)S(1)} %get-tuple-element.50), channel_id=1, source_target_pairs={{0,8},{8,16},{16,24},{24,32},{32,40},{40,48},{48,56},{1,9},{9,17},... | collective-permute-start | bytes 393224 | tf_op jit(solution)/shard_map/ppermute | solution.py:15
  226.3 1.4 collective-permute-done.21
  229.4 1.9 collective-permute-start.26
  231.4 3.6 %collective-permute-start.27 = (f32[8,1,1024]{2,1,0:T(1,128)S(1)}, f32[8,1,1024]{2,1,0:T(1,128)S(1)}, u32[]{:S(2)}, u32[]{:S(2)}) collective-permute-start(f32[8,1,1024]{2,1,0:T(1,128)S(1)} %get-tuple-element.118), channel_id=1, source_target_pairs={{0,1},{1,2},{2,3},{3,4},{4,5},{5,6},{6,7},{8,9},{9,10},{10,11},{11... | collective-permute-start | bytes 98312 | tf_op jit(solution)/shard_map/ppermute | solution.py:15
  235.2 1.3 collective-permute-start.24
  236.5 5.4 %collective-permute-start.25 = (f32[1,8,1024]{2,1,0:T(8,128)S(1)}, f32[1,8,1024]{2,1,0:T(8,128)S(1)}, u32[]{:S(2)}, u32[]{:S(2)}) collective-permute-start(f32[1,8,1024]{2,1,0:T(8,128)S(1)} %get-tuple-element.114), channel_id=1, source_target_pairs={{0,8},{8,16},{16,24},{24,32},{32,40},{40,48},{48,56},{1,9},{9,17},... | collective-permute-start | bytes 98312 | tf_op jit(solution)/shard_map/ppermute | solution.py:15
  244.6 1.9 collective-permute-start.30
  246.5 3.6 %collective-permute-start.31 = (f32[4,8,1,1024]{3,2,1,0:T(1,128)S(1)}, f32[4,8,1,1024]{3,2,1,0:T(1,128)S(1)}, u32[]{:S(2)}, u32[]{:S(2)}) collective-permute-start(f32[4,8,1,1024]{3,2,1,0:T(1,128)S(1)} %get-tuple-element.40), channel_id=1, source_target_pairs={{0,1},{1,2},{2,3},{3,4},{4,5},{5,6},{6,7},{8,9},{9,10},{10,11},{11... | collective-permute-start | bytes 393224 | tf_op jit(solution)/shard_map/ppermute | solution.py:15
  250.2 1.3 collective-permute-start.28
  251.5 5.6 %collective-permute-start.29 = (f32[4,1,8,1024]{3,2,1,0:T(8,128)S(1)}, f32[4,1,8,1024]{3,2,1,0:T(8,128)S(1)}, u32[]{:S(2)}, u32[]{:S(2)}) collective-permute-start(f32[4,1,8,1024]{3,2,1,0:T(8,128)S(1)} %get-tuple-element.36), channel_id=1, source_target_pairs={{0,8},{8,16},{16,24},{24,32},{32,40},{40,48},{48,56},{1,9},{9,17},... | collective-permute-start | bytes 393224 | tf_op jit(solution)/shard_map/ppermute | solution.py:15
  258.2 1.4 collective-permute-done.29
  260.3 1.9 collective-permute-start.34
  262.2 3.6 %collective-permute-start.35 = (f32[8,1,1024]{2,1,0:T(1,128)S(1)}, f32[8,1,1024]{2,1,0:T(1,128)S(1)}, u32[]{:S(2)}, u32[]{:S(2)}) collective-permute-start(f32[8,1,1024]{2,1,0:T(1,128)S(1)} %get-tuple-element.102), channel_id=1, source_target_pairs={{0,1},{1,2},{2,3},{3,4},{4,5},{5,6},{6,7},{8,9},{9,10},{10,11},{11... | collective-permute-start | bytes 98312 | tf_op jit(solution)/shard_map/ppermute | solution.py:15
  267.4 5.2 %collective-permute-start.33 = (f32[1,8,1024]{2,1,0:T(8,128)S(1)}, f32[1,8,1024]{2,1,0:T(8,128)S(1)}, u32[]{:S(2)}, u32[]{:S(2)}) collective-permute-start(f32[1,8,1024]{2,1,0:T(8,128)S(1)} %get-tuple-element.98), channel_id=1, source_target_pairs={{0,8},{8,16},{16,24},{24,32},{32,40},{40,48},{48,56},{1,9},{9,17},... | collective-permute-start | bytes 98312 | tf_op jit(solution)/shard_map/ppermute | solution.py:15
  274.5 1.4 fusion.27
  277.0 30.5 %reduce-scatter.2.cloned.1.call-done = f32[4,8,8,512]{3,2,1,0:T(8,128)} async-done(((f32[4,8,8,1024]{3,2,1,0:T(8,128)}), f32[4,8,8,512]{3,2,1,0:T(8,128)}) %reduce-scatter.2.cloned.1.call-update) | async-done | bytes 524304 | tf_op jit(solution)/shard_map/reduce_scatter | solution.py:133
  (209 shorter events, 37.2 us)
Async XLA Ops:
  7.2 300.3 %reduce-scatter.2.cloned.1.call-start = ((), (), s32[]{:S(2)}) async-start(), calls=%async_computation.1 | async-start | bytes 1572864 | tf_op jit(solution)/shard_map/reduce_scatter | solution.py:133
  7.2 23.0 %copy-start.3 = (bf16[4,4,8,8,1024]{4,3,2,1,0:T(8,128)(2,1)S(1)}, bf16[4,4,8,8,1024]{4,3,2,1,0:T(8,128)(2,1)}, u32[]{:S(2)}) copy-start(bf16[4,4,8,8,1024]{4,3,2,1,0:T(8,128)(2,1)} %param.12) | copy-start | bytes 6291460
  9.3 14.4 %copy-start = (f32[1,4,8,8,1024]{4,3,2,1,0:T(8,128)S(1)}, f32[1,4,8,8,1024]{4,3,2,1,0:T(8,128)}, u32[]{:S(2)}) copy-start(f32[1,4,8,8,1024]{4,3,2,1,0:T(8,128)} %param.13) | copy-start | bytes 3145732
  9.3 140.5 %collective-permute-start.4 = (bf16[4,4,1,8,1024]{4,3,1,2,0:T(8,128)(2,1)}, bf16[4,4,1,8,1024]{4,3,1,2,0:T(8,128)(2,1)}, u32[]{:S(2)}, u32[]{:S(2)}) collective-permute-start(bf16[4,4,1,8,1024]{4,3,1,2,0:T(8,128)(2,1)} %get-tuple-element.31), channel_id=1, source_target_pairs={{8,0},{16,8},{24,16},{32,24},{40,32},{48,40},{56,48},{9,1},{17,9},... | collective-permute-start | bytes 786440 | tf_op jit(solution)/shard_map/ppermute | solution.py:16
  10.7 140.1 %collective-permute-start.5 = (bf16[4,4,1,8,1024]{4,3,1,2,0:T(8,128)(2,1)}, bf16[4,4,1,8,1024]{4,3,1,2,0:T(8,128)(2,1)}, u32[]{:S(2)}, u32[]{:S(2)}) collective-permute-start(bf16[4,4,1,8,1024]{4,3,1,2,0:T(8,128)(2,1)} %get-tuple-element.30), channel_id=1, source_target_pairs={{0,8},{8,16},{16,24},{24,32},{32,40},{40,48},{48,56},{1,9},{9,17},... | collective-permute-start | bytes 786440 | tf_op jit(solution)/shard_map/ppermute | solution.py:15
  20.4 131.7 %collective-permute-start.6 = (bf16[4,4,8,1,1024]{4,3,2,1,0:T(2,128)(2,1)}, bf16[4,4,8,1,1024]{4,3,2,1,0:T(2,128)(2,1)}, u32[]{:S(2)}, u32[]{:S(2)}) collective-permute-start(bf16[4,4,8,1,1024]{4,3,2,1,0:T(2,128)(2,1)} %get-tuple-element.33), channel_id=1, source_target_pairs={{1,0},{2,1},{3,2},{4,3},{5,4},{6,5},{7,6},{9,8},{10,9},{11,10},{12... | collective-permute-start | bytes 786440 | tf_op jit(solution)/shard_map/ppermute | solution.py:16
  24.6 114.7 %collective-permute-start.2 = (f32[4,8,1,1024]{3,2,1,0:T(1,128)}, f32[4,8,1,1024]{3,2,1,0:T(1,128)}, u32[]{:S(2)}, u32[]{:S(2)}) collective-permute-start(f32[4,8,1,1024]{3,2,1,0:T(1,128)} %get-tuple-element.83), channel_id=1, source_target_pairs={{1,0},{2,1},{3,2},{4,3},{5,4},{6,5},{7,6},{9,8},{10,9},{11,10},{12... | collective-permute-start | bytes 393224 | tf_op jit(solution)/shard_map/ppermute | solution.py:16
  26.5 114.1 %collective-permute-start.3 = (f32[4,8,1,1024]{3,2,1,0:T(1,128)}, f32[4,8,1,1024]{3,2,1,0:T(1,128)}, u32[]{:S(2)}, u32[]{:S(2)}) collective-permute-start(f32[4,8,1,1024]{3,2,1,0:T(1,128)} %get-tuple-element.82), channel_id=1, source_target_pairs={{0,1},{1,2},{2,3},{3,4},{4,5},{5,6},{6,7},{8,9},{9,10},{10,11},{11... | collective-permute-start | bytes 393224 | tf_op jit(solution)/shard_map/ppermute | solution.py:15
  30.6 4.5 %copy-start.1 = (f32[4,8,8,1024]{3,2,1,0:T(8,128)}, f32[4,8,8,1024]{3,2,1,0:T(8,128)S(1)}, u32[]{:S(2)}) copy-start(f32[4,8,8,1024]{3,2,1,0:T(8,128)S(1)} %get-tuple-element.23) | copy-start | bytes 3145732
  35.0 2.2 copy-start.32
  35.0 2.2 copy-start.33
  41.4 1.5 copy-start.2
  48.1 2.2 copy-start.34
  50.3 11.4 %copy-start.35 = (s32[3]{0:T(128)S(1)}, s32[3]{0:T(128)}, u32[]{:S(2)}) copy-start(s32[3]{0:T(128)} %constant.65.clone.1) | copy-start | bytes 40
  56.0 76.3 %copy-start.31 = (f32[3,1024]{1,0:T(4,128)S(1)}, f32[3,1024]{1,0:T(4,128)}, u32[]{:S(2)}) copy-start(f32[3,1024]{1,0:T(4,128)} %param.11) | copy-start | bytes 36868
  138.6 2.0 copy-start.30
  138.6 6.0 %copy-start.9 = (f32[4,8,7,1024]{3,2,1,0:T(8,128)S(1)}, f32[4,8,7,1024]{3,2,1,0:T(8,128)}, u32[]{:S(2)}) copy-start(f32[4,8,7,1024]{3,2,1,0:T(8,128)} %get-tuple-element.84) | copy-start | bytes 2752516
  138.7 6.0 %copy-start.10 = (f32[4,8,7,1024]{3,2,1,0:T(8,128)S(1)}, f32[4,8,7,1024]{3,2,1,0:T(8,128)}, u32[]{:S(2)}) copy-start(f32[4,8,7,1024]{3,2,1,0:T(8,128)} %get-tuple-element.85) | copy-start | bytes 2752516
  139.3 7.0 %collective-permute-start = (f32[4,1,8,1024]{3,2,1,0:T(8,128)}, f32[4,1,8,1024]{3,2,1,0:T(8,128)S(1)}, u32[]{:S(2)}, u32[]{:S(2)}) collective-permute-start(f32[4,1,8,1024]{3,2,1,0:T(8,128)} %get-tuple-element.79), channel_id=1, source_target_pairs={{8,0},{16,8},{24,16},{32,24},{40,32},{48,40},{56,48},{9,1},{17,9},... | collective-permute-start | bytes 393224 | tf_op jit(solution)/shard_map/ppermute | solution.py:16
  140.6 8.9 %collective-permute-start.1 = (f32[4,1,8,1024]{3,2,1,0:T(8,128)S(1)}, f32[4,1,8,1024]{3,2,1,0:T(8,128)S(1)}, u32[]{:S(2)}, u32[]{:S(2)}) collective-permute-start(f32[4,1,8,1024]{3,2,1,0:T(8,128)S(1)} %copy-done.30), channel_id=1, source_target_pairs={{0,8},{8,16},{16,24},{24,32},{32,40},{40,48},{48,56},{1,9},{9,17},... | collective-permute-start | bytes 393224 | tf_op jit(solution)/shard_map/ppermute | solution.py:15
  144.6 1.6 copy-start.29
  144.6 4.9 %copy-start.27 = (f32[4,7,8,1024]{3,2,1,0:T(8,128)S(1)}, f32[4,7,8,1024]{3,2,1,0:T(8,128)}, u32[]{:S(2)}) copy-start(f32[4,7,8,1024]{3,2,1,0:T(8,128)} %get-tuple-element.80) | copy-start | bytes 2752516
  144.6 4.9 %copy-start.28 = (f32[4,7,8,1024]{3,2,1,0:T(8,128)S(1)}, f32[4,7,8,1024]{3,2,1,0:T(8,128)}, u32[]{:S(2)}) copy-start(f32[4,7,8,1024]{3,2,1,0:T(8,128)} %get-tuple-element.81) | copy-start | bytes 2752516
  146.3 9.4 %collective-permute-start.7 = (bf16[4,4,8,1,1024]{4,3,2,1,0:T(2,128)(2,1)S(1)}, bf16[4,4,8,1,1024]{4,3,2,1,0:T(2,128)(2,1)S(1)}, u32[]{:S(2)}, u32[]{:S(2)}) collective-permute-start(bf16[4,4,8,1,1024]{4,3,2,1,0:T(2,128)(2,1)S(1)} %copy-done.29), channel_id=1, source_target_pairs={{0,1},{1,2},{2,3},{3,4},{4,5},{5,6},{6,7},{8,9},{9,10},{10,11},{11... | collective-permute-start | bytes 786440 | tf_op jit(solution)/shard_map/ppermute | solution.py:15
  149.6 2.3 copy-start.26
  149.8 2.1 copy-start.25
  152.1 4.0 %copy-start.15 = (f32[4,8,7,1024]{3,2,1,0:T(8,128)S(1)}, f32[4,8,7,1024]{3,2,1,0:T(8,128)}, u32[]{:S(2)}) copy-start(f32[4,8,7,1024]{3,2,1,0:T(8,128)} %get-tuple-element.159) | copy-start | bytes 2752516
  152.1 4.0 %copy-start.16 = (f32[4,8,7,1024]{3,2,1,0:T(8,128)S(1)}, f32[4,8,7,1024]{3,2,1,0:T(8,128)}, u32[]{:S(2)}) copy-start(f32[4,8,7,1024]{3,2,1,0:T(8,128)} %get-tuple-element.160) | copy-start | bytes 2752516
  156.2 1.5 copy-start.7
  156.2 1.6 copy-start.8
  158.1 6.6 %copy-start.19 = (f32[4,7,8,1024]{3,2,1,0:T(8,128)S(1)}, f32[4,7,8,1024]{3,2,1,0:T(8,128)}, u32[]{:S(2)}) copy-start(f32[4,7,8,1024]{3,2,1,0:T(8,128)} %get-tuple-element.72) | copy-start | bytes 2752516
  158.1 6.6 %copy-start.20 = (f32[4,7,8,1024]{3,2,1,0:T(8,128)S(1)}, f32[4,7,8,1024]{3,2,1,0:T(8,128)}, u32[]{:S(2)}) copy-start(f32[4,7,8,1024]{3,2,1,0:T(8,128)} %get-tuple-element.73) | copy-start | bytes 2752516
  158.2 20.7 %collective-permute-start.10 = (f32[8,1,1024]{2,1,0:T(1,128)S(1)}, f32[8,1,1024]{2,1,0:T(1,128)S(1)}, u32[]{:S(2)}, u32[]{:S(2)}) collective-permute-start(f32[8,1,1024]{2,1,0:T(1,128)S(1)} %get-tuple-element.135), channel_id=1, source_target_pairs={{1,0},{2,1},{3,2},{4,3},{5,4},{6,5},{7,6},{9,8},{10,9},{11,10},{12... | collective-permute-start | bytes 98312 | tf_op jit(solution)/shard_map/ppermute | solution.py:16
  160.3 18.6 %collective-permute-start.11 = (f32[8,1,1024]{2,1,0:T(1,128)S(1)}, f32[8,1,1024]{2,1,0:T(1,128)S(1)}, u32[]{:S(2)}, u32[]{:S(2)}) collective-permute-start(f32[8,1,1024]{2,1,0:T(1,128)S(1)} %get-tuple-element.134), channel_id=1, source_target_pairs={{0,1},{1,2},{2,3},{3,4},{4,5},{5,6},{6,7},{8,9},{9,10},{10,11},{11... | collective-permute-start | bytes 98312 | tf_op jit(solution)/shard_map/ppermute | solution.py:15
  164.7 1.5 copy-start.12
  166.3 1.5 copy-start.24
  167.7 1.5 copy-start.18
  170.7 1.5 copy-start.14
  172.9 6.1 %collective-permute-start.8 = (f32[1,8,1024]{2,1,0:T(8,128)S(1)}, f32[1,8,1024]{2,1,0:T(8,128)S(1)}, u32[]{:S(2)}, u32[]{:S(2)}) collective-permute-start(f32[1,8,1024]{2,1,0:T(8,128)S(1)} %get-tuple-element.131), channel_id=1, source_target_pairs={{8,0},{16,8},{24,16},{32,24},{40,32},{48,40},{56,48},{9,1},{17,9},... | collective-permute-start | bytes 98312 | tf_op jit(solution)/shard_map/ppermute | solution.py:16
  174.2 5.7 %collective-permute-start.9 = (f32[1,8,1024]{2,1,0:T(8,128)S(1)}, f32[1,8,1024]{2,1,0:T(8,128)S(1)}, u32[]{:S(2)}, u32[]{:S(2)}) collective-permute-start(f32[1,8,1024]{2,1,0:T(8,128)S(1)} %get-tuple-element.130), channel_id=1, source_target_pairs={{0,8},{8,16},{16,24},{24,32},{32,40},{40,48},{48,56},{1,9},{9,17},... | collective-permute-start | bytes 98312 | tf_op jit(solution)/shard_map/ppermute | solution.py:15
  181.5 12.6 %collective-permute-start.14 = (f32[4,8,1,1024]{3,2,1,0:T(1,128)S(1)}, f32[4,8,1,1024]{3,2,1,0:T(1,128)S(1)}, u32[]{:S(2)}, u32[]{:S(2)}) collective-permute-start(f32[4,8,1,1024]{3,2,1,0:T(1,128)S(1)} %get-tuple-element.69), channel_id=1, source_target_pairs={{1,0},{2,1},{3,2},{4,3},{5,4},{6,5},{7,6},{9,8},{10,9},{11,10},{12... | collective-permute-start | bytes 393224 | tf_op jit(solution)/shard_map/ppermute | solution.py:16
  183.6 10.5 %collective-permute-start.15 = (f32[4,8,1,1024]{3,2,1,0:T(1,128)S(1)}, f32[4,8,1,1024]{3,2,1,0:T(1,128)S(1)}, u32[]{:S(2)}, u32[]{:S(2)}) collective-permute-start(f32[4,8,1,1024]{3,2,1,0:T(1,128)S(1)} %get-tuple-element.68), channel_id=1, source_target_pairs={{0,1},{1,2},{2,3},{3,4},{4,5},{5,6},{6,7},{8,9},{9,10},{10,11},{11... | collective-permute-start | bytes 393224 | tf_op jit(solution)/shard_map/ppermute | solution.py:15
  187.3 7.3 %collective-permute-start.12 = (f32[4,1,8,1024]{3,2,1,0:T(8,128)S(1)}, f32[4,1,8,1024]{3,2,1,0:T(8,128)S(1)}, u32[]{:S(2)}, u32[]{:S(2)}) collective-permute-start(f32[4,1,8,1024]{3,2,1,0:T(8,128)S(1)} %get-tuple-element.65), channel_id=1, source_target_pairs={{8,0},{16,8},{24,16},{32,24},{40,32},{48,40},{56,48},{9,1},{17,9},... | collective-permute-start | bytes 393224 | tf_op jit(solution)/shard_map/ppermute | solution.py:16
  188.6 7.4 %collective-permute-start.13 = (f32[4,1,8,1024]{3,2,1,0:T(8,128)S(1)}, f32[4,1,8,1024]{3,2,1,0:T(8,128)S(1)}, u32[]{:S(2)}, u32[]{:S(2)}) collective-permute-start(f32[4,1,8,1024]{3,2,1,0:T(8,128)S(1)} %get-tuple-element.64), channel_id=1, source_target_pairs={{0,8},{8,16},{16,24},{24,32},{32,40},{40,48},{48,56},{1,9},{9,17},... | collective-permute-start | bytes 393224 | tf_op jit(solution)/shard_map/ppermute | solution.py:15
  197.7 12.3 %collective-permute-start.18 = (f32[8,1,1024]{2,1,0:T(1,128)S(1)}, f32[8,1,1024]{2,1,0:T(1,128)S(1)}, u32[]{:S(2)}, u32[]{:S(2)}) collective-permute-start(f32[8,1,1024]{2,1,0:T(1,128)S(1)} %get-tuple-element.127), channel_id=1, source_target_pairs={{1,0},{2,1},{3,2},{4,3},{5,4},{6,5},{7,6},{9,8},{10,9},{11,10},{12... | collective-permute-start | bytes 98312 | tf_op jit(solution)/shard_map/ppermute | solution.py:16
  199.6 10.4 %collective-permute-start.19 = (f32[8,1,1024]{2,1,0:T(1,128)S(1)}, f32[8,1,1024]{2,1,0:T(1,128)S(1)}, u32[]{:S(2)}, u32[]{:S(2)}) collective-permute-start(f32[8,1,1024]{2,1,0:T(1,128)S(1)} %get-tuple-element.126), channel_id=1, source_target_pairs={{0,1},{1,2},{2,3},{3,4},{4,5},{5,6},{6,7},{8,9},{9,10},{10,11},{11... | collective-permute-start | bytes 98312 | tf_op jit(solution)/shard_map/ppermute | solution.py:15
  203.7 6.4 %collective-permute-start.16 = (f32[1,8,1024]{2,1,0:T(8,128)S(1)}, f32[1,8,1024]{2,1,0:T(8,128)S(1)}, u32[]{:S(2)}, u32[]{:S(2)}) collective-permute-start(f32[1,8,1024]{2,1,0:T(8,128)S(1)} %get-tuple-element.123), channel_id=1, source_target_pairs={{8,0},{16,8},{24,16},{32,24},{40,32},{48,40},{56,48},{9,1},{17,9},... | collective-permute-start | bytes 98312 | tf_op jit(solution)/shard_map/ppermute | solution.py:16
  205.0 6.0 %collective-permute-start.17 = (f32[1,8,1024]{2,1,0:T(8,128)S(1)}, f32[1,8,1024]{2,1,0:T(8,128)S(1)}, u32[]{:S(2)}, u32[]{:S(2)}) collective-permute-start(f32[1,8,1024]{2,1,0:T(8,128)S(1)} %get-tuple-element.122), channel_id=1, source_target_pairs={{0,8},{8,16},{16,24},{24,32},{32,40},{40,48},{48,56},{1,9},{9,17},... | collective-permute-start | bytes 98312 | tf_op jit(solution)/shard_map/ppermute | solution.py:15
  212.7 13.1 %collective-permute-start.22 = (f32[4,8,1,1024]{3,2,1,0:T(1,128)S(1)}, f32[4,8,1,1024]{3,2,1,0:T(1,128)S(1)}, u32[]{:S(2)}, u32[]{:S(2)}) collective-permute-start(f32[4,8,1,1024]{3,2,1,0:T(1,128)S(1)} %get-tuple-element.55), channel_id=1, source_target_pairs={{1,0},{2,1},{3,2},{4,3},{5,4},{6,5},{7,6},{9,8},{10,9},{11,10},{12... | collective-permute-start | bytes 393224 | tf_op jit(solution)/shard_map/ppermute | solution.py:16
  214.6 11.2 %collective-permute-start.23 = (f32[4,8,1,1024]{3,2,1,0:T(1,128)S(1)}, f32[4,8,1,1024]{3,2,1,0:T(1,128)S(1)}, u32[]{:S(2)}, u32[]{:S(2)}) collective-permute-start(f32[4,8,1,1024]{3,2,1,0:T(1,128)S(1)} %get-tuple-element.54), channel_id=1, source_target_pairs={{0,1},{1,2},{2,3},{3,4},{4,5},{5,6},{6,7},{8,9},{9,10},{10,11},{11... | collective-permute-start | bytes 393224 | tf_op jit(solution)/shard_map/ppermute | solution.py:15
  218.3 8.0 %collective-permute-start.20 = (f32[4,1,8,1024]{3,2,1,0:T(8,128)S(1)}, f32[4,1,8,1024]{3,2,1,0:T(8,128)S(1)}, u32[]{:S(2)}, u32[]{:S(2)}) collective-permute-start(f32[4,1,8,1024]{3,2,1,0:T(8,128)S(1)} %get-tuple-element.51), channel_id=1, source_target_pairs={{8,0},{16,8},{24,16},{32,24},{40,32},{48,40},{56,48},{9,1},{17,9},... | collective-permute-start | bytes 393224 | tf_op jit(solution)/shard_map/ppermute | solution.py:16
  219.6 8.2 %collective-permute-start.21 = (f32[4,1,8,1024]{3,2,1,0:T(8,128)S(1)}, f32[4,1,8,1024]{3,2,1,0:T(8,128)S(1)}, u32[]{:S(2)}, u32[]{:S(2)}) collective-permute-start(f32[4,1,8,1024]{3,2,1,0:T(8,128)S(1)} %get-tuple-element.50), channel_id=1, source_target_pairs={{0,8},{8,16},{16,24},{24,32},{32,40},{40,48},{48,56},{1,9},{9,17},... | collective-permute-start | bytes 393224 | tf_op jit(solution)/shard_map/ppermute | solution.py:15
  229.4 12.5 %collective-permute-start.26 = (f32[8,1,1024]{2,1,0:T(1,128)S(1)}, f32[8,1,1024]{2,1,0:T(1,128)S(1)}, u32[]{:S(2)}, u32[]{:S(2)}) collective-permute-start(f32[8,1,1024]{2,1,0:T(1,128)S(1)} %get-tuple-element.119), channel_id=1, source_target_pairs={{1,0},{2,1},{3,2},{4,3},{5,4},{6,5},{7,6},{9,8},{10,9},{11,10},{12... | collective-permute-start | bytes 98312 | tf_op jit(solution)/shard_map/ppermute | solution.py:16
  231.4 10.6 %collective-permute-start.27 = (f32[8,1,1024]{2,1,0:T(1,128)S(1)}, f32[8,1,1024]{2,1,0:T(1,128)S(1)}, u32[]{:S(2)}, u32[]{:S(2)}) collective-permute-start(f32[8,1,1024]{2,1,0:T(1,128)S(1)} %get-tuple-element.118), channel_id=1, source_target_pairs={{0,1},{1,2},{2,3},{3,4},{4,5},{5,6},{6,7},{8,9},{9,10},{10,11},{11... | collective-permute-start | bytes 98312 | tf_op jit(solution)/shard_map/ppermute | solution.py:15
  235.2 6.9 %collective-permute-start.24 = (f32[1,8,1024]{2,1,0:T(8,128)S(1)}, f32[1,8,1024]{2,1,0:T(8,128)S(1)}, u32[]{:S(2)}, u32[]{:S(2)}) collective-permute-start(f32[1,8,1024]{2,1,0:T(8,128)S(1)} %get-tuple-element.115), channel_id=1, source_target_pairs={{8,0},{16,8},{24,16},{32,24},{40,32},{48,40},{56,48},{9,1},{17,9},... | collective-permute-start | bytes 98312 | tf_op jit(solution)/shard_map/ppermute | solution.py:16
  236.5 6.4 %collective-permute-start.25 = (f32[1,8,1024]{2,1,0:T(8,128)S(1)}, f32[1,8,1024]{2,1,0:T(8,128)S(1)}, u32[]{:S(2)}, u32[]{:S(2)}) collective-permute-start(f32[1,8,1024]{2,1,0:T(8,128)S(1)} %get-tuple-element.114), channel_id=1, source_target_pairs={{0,8},{8,16},{16,24},{24,32},{32,40},{40,48},{48,56},{1,9},{9,17},... | collective-permute-start | bytes 98312 | tf_op jit(solution)/shard_map/ppermute | solution.py:15
  244.6 13.1 %collective-permute-start.30 = (f32[4,8,1,1024]{3,2,1,0:T(1,128)S(1)}, f32[4,8,1,1024]{3,2,1,0:T(1,128)S(1)}, u32[]{:S(2)}, u32[]{:S(2)}) collective-permute-start(f32[4,8,1,1024]{3,2,1,0:T(1,128)S(1)} %get-tuple-element.41), channel_id=1, source_target_pairs={{1,0},{2,1},{3,2},{4,3},{5,4},{6,5},{7,6},{9,8},{10,9},{11,10},{12... | collective-permute-start | bytes 393224 | tf_op jit(solution)/shard_map/ppermute | solution.py:16
  246.5 11.2 %collective-permute-start.31 = (f32[4,8,1,1024]{3,2,1,0:T(1,128)S(1)}, f32[4,8,1,1024]{3,2,1,0:T(1,128)S(1)}, u32[]{:S(2)}, u32[]{:S(2)}) collective-permute-start(f32[4,8,1,1024]{3,2,1,0:T(1,128)S(1)} %get-tuple-element.40), channel_id=1, source_target_pairs={{0,1},{1,2},{2,3},{3,4},{4,5},{5,6},{6,7},{8,9},{9,10},{10,11},{11... | collective-permute-start | bytes 393224 | tf_op jit(solution)/shard_map/ppermute | solution.py:15
  250.2 8.0 %collective-permute-start.28 = (f32[4,1,8,1024]{3,2,1,0:T(8,128)S(1)}, f32[4,1,8,1024]{3,2,1,0:T(8,128)S(1)}, u32[]{:S(2)}, u32[]{:S(2)}) collective-permute-start(f32[4,1,8,1024]{3,2,1,0:T(8,128)S(1)} %get-tuple-element.37), channel_id=1, source_target_pairs={{8,0},{16,8},{24,16},{32,24},{40,32},{48,40},{56,48},{9,1},{17,9},... | collective-permute-start | bytes 393224 | tf_op jit(solution)/shard_map/ppermute | solution.py:16
  251.5 8.2 %collective-permute-start.29 = (f32[4,1,8,1024]{3,2,1,0:T(8,128)S(1)}, f32[4,1,8,1024]{3,2,1,0:T(8,128)S(1)}, u32[]{:S(2)}, u32[]{:S(2)}) collective-permute-start(f32[4,1,8,1024]{3,2,1,0:T(8,128)S(1)} %get-tuple-element.36), channel_id=1, source_target_pairs={{0,8},{8,16},{16,24},{24,32},{32,40},{40,48},{48,56},{1,9},{9,17},... | collective-permute-start | bytes 393224 | tf_op jit(solution)/shard_map/ppermute | solution.py:15
  260.3 12.3 %collective-permute-start.34 = (f32[8,1,1024]{2,1,0:T(1,128)S(1)}, f32[8,1,1024]{2,1,0:T(1,128)S(1)}, u32[]{:S(2)}, u32[]{:S(2)}) collective-permute-start(f32[8,1,1024]{2,1,0:T(1,128)S(1)} %get-tuple-element.103), channel_id=1, source_target_pairs={{1,0},{2,1},{3,2},{4,3},{5,4},{6,5},{7,6},{9,8},{10,9},{11,10},{12... | collective-permute-start | bytes 98312 | tf_op jit(solution)/shard_map/ppermute | solution.py:16
  262.2 10.4 %collective-permute-start.35 = (f32[8,1,1024]{2,1,0:T(1,128)S(1)}, f32[8,1,1024]{2,1,0:T(1,128)S(1)}, u32[]{:S(2)}, u32[]{:S(2)}) collective-permute-start(f32[8,1,1024]{2,1,0:T(1,128)S(1)} %get-tuple-element.102), channel_id=1, source_target_pairs={{0,1},{1,2},{2,3},{3,4},{4,5},{5,6},{6,7},{8,9},{9,10},{10,11},{11... | collective-permute-start | bytes 98312 | tf_op jit(solution)/shard_map/ppermute | solution.py:15
  266.1 6.6 %collective-permute-start.32 = (f32[1,8,1024]{2,1,0:T(8,128)S(1)}, f32[1,8,1024]{2,1,0:T(8,128)S(1)}, u32[]{:S(2)}, u32[]{:S(2)}) collective-permute-start(f32[1,8,1024]{2,1,0:T(8,128)S(1)} %get-tuple-element.99), channel_id=1, source_target_pairs={{8,0},{16,8},{24,16},{32,24},{40,32},{48,40},{56,48},{9,1},{17,9},... | collective-permute-start | bytes 98312 | tf_op jit(solution)/shard_map/ppermute | solution.py:16
  267.4 6.2 %collective-permute-start.33 = (f32[1,8,1024]{2,1,0:T(8,128)S(1)}, f32[1,8,1024]{2,1,0:T(8,128)S(1)}, u32[]{:S(2)}, u32[]{:S(2)}) collective-permute-start(f32[1,8,1024]{2,1,0:T(8,128)S(1)} %get-tuple-element.98), channel_id=1, source_target_pairs={{0,8},{8,16},{16,24},{24,32},{32,40},{40,48},{48,56},{1,9},{9,17},... | collective-permute-start | bytes 98312 | tf_op jit(solution)/shard_map/ppermute | solution.py:15
  (9 other events, 11.2 us)
Sparse Core Ops, SparseCore 0:
  276.1 31.3 reduce-scatter.1
where the time goes:
time: 316 us; the launch traced here: 314 us
  starting transfers between devices  110 us (35%)
  blocking collectives  66.1 us (21%)
  local copies, waits for them, and re-layouts  42.6 us (13%)
  waiting for transfers between devices  40 us (13%)
  other arithmetic  39.5 us (12%)
  between operations  16.2 us (5%)
    ppermute x18, starting transfers between devices, neighbours(): before = lax.ppermute(last, axis, up)  79.1 us
    psum x1, blocking collectives, shards(): samples = lax.psum(slot.at[me].set(local_samples), ('pair', 'gx', 'gy'))[me]  66.1 us
    ppermute x18, starting transfers between devices, neighbours(): after = lax.ppermute(first, axis, down)  30.7 us
    reduce_scatter x1, waiting for transfers between devices, shards(): lax.psum_scatter(kernel_local, 'pair', scatter_dimension=3, tiled=True)  30.5 us
    unnamed x73, local copies, waits for them, and re-layouts  11.4 us
    gather x4, local copies, waits for them, and re-layouts, shards(): forward_field[t, 0][sx, sy, sz]  11.3 us
    ppermute x18, waiting for transfers between devices, neighbours(): before = lax.ppermute(last, axis, up)  9.45 us
    scatter-add x4, other arithmetic, shards(): injected = jnp.zeros((width_x * width_y * depth,), jnp.float32).at[rcv_fl...  8.35 us
  transfers between devices with their start and end apart: 37, of which 9 were waited for; matrix products, arithmetic and copies ran while one was open for 19% of the time, Pallas kernels for 0%

commit v1 on v0

--- a/solution.py
+++ b/solution.py
@@ -80,7 +80,9 @@
     )
     me = lax.axis_index("pair")
     slot = jnp.zeros((lax.axis_size("pair"),) + local_samples.shape, jnp.float32)
-    samples = lax.psum(slot.at[me].set(local_samples), ("pair", "gx", "gy"))[me]
+    samples = jnp.sum(lax.all_gather(slot.at[me].set(local_samples), ("pair", "gx", "gy")), axis=0)[
+        me
+    ]
     forward_rims = halos(forward_field, 2, 3)
     rcv_flat = (rx * width_y + ry) * depth + rz
     state = adjoint_state[0]

time: 316 us -> 411 us (1.30)
  waiting for transfers between devices: 40 us -> 172 us
  blocking collectives: 66.1 us -> 0 us
  other arithmetic: 39.5 us -> 61.5 us
  local copies, waits for them, and re-layouts: 42.6 us -> 52.2 us
    all_gather x0 -> x1, waiting for transfers between devices: none -> 136 us  [shards(): lax.all_gather(slot.at[me].set(local_samples), ('pair', 'gx', 'gy'))]
    psum x1 -> x0, blocking collectives: 66.1 us -> none  [shards(): samples = lax.psum(slot.at[me].set(local_samples), ('pair', 'gx', 'gy'))[me]]
    ppermute x18, starting transfers between devices: 79.1 us -> 72.7 us  [neighbours(): before = lax.ppermute(last, axis, up)]
    mul x12, other arithmetic: 5.13 us -> 11.3 us  [central(): north_diff = (y_hi - y_lo) * 0.5]
    reshape x4, local copies, waits for them, and re-layouts: 0.19 us -> 5.89 us  [shards(): injected = jnp.zeros((width_x * width_y * depth,), jnp.float32).at[rcv_fl...]
    unnamed x73 -> x99, local copies, waits for them, and re-layouts: 11.4 us -> 12.7 us
  transfers between devices with their start and end apart: 37 -> 38, of which waited for: 9 -> 10; matrix products, arithmetic and copies ran while one was open for 19% -> 19% of each run, Pallas kernels for 0% -> 0%
where the time goes in v1:
time: 411 us; the launch traced here: 409 us
  waiting for transfers between devices  172 us (42%)
  starting transfers between devices  107 us (26%)
  other arithmetic  61.5 us (15%)
  local copies, waits for them, and re-layouts  52.2 us (13%)
  between operations  16.1 us (4%)
    all_gather x1, waiting for transfers between devices, shards(): lax.all_gather(slot.at[me].set(local_samples), ('pair', 'gx', 'gy'))  136 us
    ppermute x18, starting transfers between devices, neighbours(): before = lax.ppermute(last, axis, up)  72.7 us
    ppermute x18, starting transfers between devices, neighbours(): after = lax.ppermute(first, axis, down)  34 us
    reduce_scatter x1, waiting for transfers between devices, shards(): lax.psum_scatter(kernel_local, 'pair', scatter_dimension=3, tiled=True)  29.2 us
    unnamed x99, local copies, waits for them, and re-layouts  12.7 us
    mul x12, other arithmetic, central(): north_diff = (y_hi - y_lo) * 0.5  11.3 us
    gather x4, local copies, waits for them, and re-layouts, shards(): forward_field[t, 0][sx, sy, sz]  11.2 us
    scatter-add x4, other arithmetic, shards(): injected = jnp.zeros((width_x * width_y * depth,), jnp.float32).at[rcv_fl...  10.6 us
  transfers between devices with their start and end apart: 38, of which 10 were waited for; matrix products, arithmetic and copies ran while one was open for 19% of the time, Pallas kernels for 0%

profile of v1, /device:TPU:1, one launch (start us, length us, event | category | flops | bytes accessed | tf_op | source)
XLA Modules:
  0.0 408.9 jit_solution(1500865470738635312)
XLA Ops:
  7.2 1.9 slice_bitcast_fusion.32
  9.1 1.4 collective-permute-start.4
  10.5 4.6 %collective-permute-start.5 = (bf16[4,4,1,8,1024]{4,3,1,2,0:T(8,128)(2,1)}, bf16[4,4,1,8,1024]{4,3,1,2,0:T(8,128)(2,1)S(1)}, u32[]{:S(2)}, u32[]{:S(2)}) collective-permute-start(bf16[4,4,1,8,1024]{4,3,1,2,0:T(8,128)(2,1)} %get-tuple-element.30), channel_id=1, source_target_pairs={{0,8},{8,16},{16,24},{24,32},{32,40},{40,48},{48,56},{1,9},{9,17},... | collective-permute-start | bytes 786440 | tf_op jit(solution)/shard_map/ppermute | solution.py:15
  15.1 4.4 %fusion.266 = (bf16[4,4,8,1,1024]{4,3,2,1,0:T(2,128)(2,1)}, bf16[4,4,8,1,1024]{4,3,2,1,0:T(2,128)(2,1)}) fusion(bf16[4,4,8,8,1024]{4,3,2,1,0:T(8,128)(2,1)} %param.12), kind=kLoop, calls=%fused_computation.506 | loop fusion | bytes 1048576 | tf_op jit(solution)/shard_map/slice | solution.py:13
  19.5 3.3 collective-permute-start.6
  25.1 2.8 gather_fusion.3
  27.9 2.8 gather_fusion.2
  30.7 2.8 gather_fusion.1
  33.5 2.8 gather_fusion
  39.2 1.9 collective-permute-start.2
  41.2 3.6 collective-permute-start.3
  44.8 2.0 bitcast_convert_fusion
  46.8 2.5 fusion.1
  49.3 1.9 fusion.271
  51.2 2.2 fusion.272
  55.3 1.5 fusion.274
  56.8 1.6 fusion.7
  58.4 1.6 fusion.11
  60.0 2.0 fusion.267
  62.0 2.3 fusion.268
  66.5 1.6 fusion.15
  69.4 4.7 %collective-permute-start.1 = (f32[4,1,8,1024]{3,2,1,0:T(8,128)S(1)}, f32[4,1,8,1024]{3,2,1,0:T(8,128)S(1)}, u32[]{:S(2)}, u32[]{:S(2)}) collective-permute-start(f32[4,1,8,1024]{3,2,1,0:T(8,128)S(1)} %copy-done.38), channel_id=1, source_target_pairs={{0,8},{8,16},{16,24},{24,32},{32,40},{40,48},{48,56},{1,9},{9,17},... | collective-permute-start | bytes 393224 | tf_op jit(solution)/shard_map/ppermute | solution.py:15
  74.2 2.5 fusion.23
  76.8 2.7 collective-permute-start.7
  83.2 1.8 fusion.231
  86.1 1.4 fusion.25
  89.6 1.5 fusion.31
  92.8 1.4 fusion.35
  96.0 1.4 fusion.39
  97.4 135.7 %all-gather.2.cloned.1.call-done = f32[128,2,4,256]{3,2,1,0:T(4,128)} async-done(((f32[1,2,4,256]{3,2,1,0:T(4,128)}), f32[128,2,4,256]{3,2,1,0:T(4,128)}) %all-gather.2.cloned.1.call-update) | async-done | bytes 1048592 | tf_op jit(solution)/shard_map/all_gather | solution.py:83
  233.1 1.4 reduce_sum.9
  235.2 2.2 scatter_custom_fusion
  238.1 2.7 fusion.217
  243.2 3.1 collective-permute-start.10
  246.3 2.5 collective-permute-start.11
  251.0 4.0 collective-permute-start.9
  255.0 2.8 scatter_custom_fusion.1
  257.8 1.7 reshape.925
  259.5 2.8 scatter_custom_fusion.2
  262.3 1.7 reshape.926
  264.0 2.8 scatter_custom_fusion.3
  266.8 1.7 reshape.927
  271.0 1.9 fusion.63
  275.1 3.2 collective-permute-start.14
  278.3 2.3 collective-permute-start.15
  281.9 4.1 collective-permute-start.13
  290.9 3.0 collective-permute-start.18
  293.9 2.5 collective-permute-start.19
  298.0 5.5 %collective-permute-start.17 = (f32[1,8,1024]{2,1,0:T(8,128)S(1)}, f32[1,8,1024]{2,1,0:T(8,128)S(1)}, u32[]{:S(2)}, u32[]{:S(2)}) collective-permute-start(f32[1,8,1024]{2,1,0:T(8,128)S(1)} %get-tuple-element.122), channel_id=1, source_target_pairs={{0,8},{8,16},{16,24},{24,32},{32,40},{40,48},{48,56},{1,9},{9,17},... | collective-permute-start | bytes 98312 | tf_op jit(solution)/shard_map/ppermute | solution.py:15
  306.3 1.9 collective-permute-start.22
  308.2 3.6 collective-permute-start.23
  313.1 5.4 %collective-permute-start.21 = (f32[4,1,8,1024]{3,2,1,0:T(8,128)S(1)}, f32[4,1,8,1024]{3,2,1,0:T(8,128)S(1)}, u32[]{:S(2)}, u32[]{:S(2)}) collective-permute-start(f32[4,1,8,1024]{3,2,1,0:T(8,128)S(1)} %get-tuple-element.50), channel_id=1, source_target_pairs={{0,8},{8,16},{16,24},{24,32},{32,40},{40,48},{48,56},{1,9},{9,17},... | collective-permute-start | bytes 393224 | tf_op jit(solution)/shard_map/ppermute | solution.py:15
  319.7 1.4 collective-permute-done.21
  323.1 1.9 collective-permute-start.26
  325.1 3.6 collective-permute-start.27
  330.2 5.5 %collective-permute-start.25 = (f32[1,8,1024]{2,1,0:T(8,128)S(1)}, f32[1,8,1024]{2,1,0:T(8,128)S(1)}, u32[]{:S(2)}, u32[]{:S(2)}) collective-permute-start(f32[1,8,1024]{2,1,0:T(8,128)S(1)} %get-tuple-element.114), channel_id=1, source_target_pairs={{0,8},{8,16},{16,24},{24,32},{32,40},{40,48},{48,56},{1,9},{9,17},... | collective-permute-start | bytes 98312 | tf_op jit(solution)/shard_map/ppermute | solution.py:15
  338.4 1.9 collective-permute-start.30
  340.3 3.6 collective-permute-start.31
  345.3 5.3 %collective-permute-start.29 = (f32[4,1,8,1024]{3,2,1,0:T(8,128)S(1)}, f32[4,1,8,1024]{3,2,1,0:T(8,128)S(1)}, u32[]{:S(2)}, u32[]{:S(2)}) collective-permute-start(f32[4,1,8,1024]{3,2,1,0:T(8,128)S(1)} %get-tuple-element.36), channel_id=1, source_target_pairs={{0,8},{8,16},{16,24},{24,32},{32,40},{40,48},{48,56},{1,9},{9,17},... | collective-permute-start | bytes 393224 | tf_op jit(solution)/shard_map/ppermute | solution.py:15
  351.7 1.4 collective-permute-done.29
  355.2 1.9 collective-permute-start.34
  357.1 3.6 collective-permute-start.35
  362.3 5.4 %collective-permute-start.33 = (f32[1,8,1024]{2,1,0:T(8,128)S(1)}, f32[1,8,1024]{2,1,0:T(8,128)S(1)}, u32[]{:S(2)}, u32[]{:S(2)}) collective-permute-start(f32[1,8,1024]{2,1,0:T(8,128)S(1)} %get-tuple-element.98), channel_id=1, source_target_pairs={{0,8},{8,16},{16,24},{24,32},{32,40},{40,48},{48,56},{1,9},{9,17},... | collective-permute-start | bytes 98312 | tf_op jit(solution)/shard_map/ppermute | solution.py:15
  372.9 29.2 %reduce-scatter.2.cloned.1.call-done = f32[4,8,8,512]{3,2,1,0:T(8,128)} async-done(((f32[4,8,8,1024]{3,2,1,0:T(8,128)}), f32[4,8,8,512]{3,2,1,0:T(8,128)}) %reduce-scatter.2.cloned.1.call-update) | async-done | bytes 524304 | tf_op jit(solution)/shard_map/reduce_scatter | solution.py:135
  (238 shorter events, 60.1 us)
Async XLA Ops:
  7.2 225.9 %all-gather.2.cloned.1.call-start = ((), (), s32[]{:S(2)}) async-start(), calls=%async_computation.1 | async-start | bytes 1056768 | tf_op jit(solution)/shard_map/all_gather | solution.py:83
  9.1 13.7 %copy-start.41 = (s32[256,3]{0,1:T(4,128)S(1)}, s32[256,3]{0,1:T(4,128)}, u32[]{:S(2)}) copy-start(s32[256,3]{0,1:T(4,128)} %param.16) | copy-start | bytes 9220
  9.1 13.7 %copy-start.42 = (s32[256,3]{0,1:T(4,128)S(1)}, s32[256,3]{0,1:T(4,128)}, u32[]{:S(2)}) copy-start(s32[256,3]{0,1:T(4,128)} %param.15) | copy-start | bytes 9220
  9.1 71.6 %collective-permute-start.4 = (bf16[4,4,1,8,1024]{4,3,1,2,0:T(8,128)(2,1)}, bf16[4,4,1,8,1024]{4,3,1,2,0:T(8,128)(2,1)}, u32[]{:S(2)}, u32[]{:S(2)}) collective-permute-start(bf16[4,4,1,8,1024]{4,3,1,2,0:T(8,128)(2,1)} %get-tuple-element.31), channel_id=1, source_target_pairs={{8,0},{16,8},{24,16},{32,24},{40,32},{48,40},{56,48},{9,1},{17,9},... | collective-permute-start | bytes 786440 | tf_op jit(solution)/shard_map/ppermute | solution.py:16
  10.5 71.3 %collective-permute-start.5 = (bf16[4,4,1,8,1024]{4,3,1,2,0:T(8,128)(2,1)}, bf16[4,4,1,8,1024]{4,3,1,2,0:T(8,128)(2,1)S(1)}, u32[]{:S(2)}, u32[]{:S(2)}) collective-permute-start(bf16[4,4,1,8,1024]{4,3,1,2,0:T(8,128)(2,1)} %get-tuple-element.30), channel_id=1, source_target_pairs={{0,8},{8,16},{16,24},{24,32},{32,40},{40,48},{48,56},{1,9},{9,17},... | collective-permute-start | bytes 786440 | tf_op jit(solution)/shard_map/ppermute | solution.py:15
  19.5 63.7 %collective-permute-start.6 = (bf16[4,4,8,1,1024]{4,3,2,1,0:T(2,128)(2,1)}, bf16[4,4,8,1,1024]{4,3,2,1,0:T(2,128)(2,1)}, u32[]{:S(2)}, u32[]{:S(2)}) collective-permute-start(bf16[4,4,8,1,1024]{4,3,2,1,0:T(2,128)(2,1)} %get-tuple-element.33), channel_id=1, source_target_pairs={{1,0},{2,1},{3,2},{4,3},{5,4},{6,5},{7,6},{9,8},{10,9},{11,10},{12... | collective-permute-start | bytes 786440 | tf_op jit(solution)/shard_map/ppermute | solution.py:16
  25.1 11.3 %copy-start.48 = (s32[3]{0:T(128)S(1)}, s32[3]{0:T(128)}, u32[]{:S(2)}) copy-start(s32[3]{0:T(128)} %constant.67.clone.1) | copy-start | bytes 40
  25.1 13.4 %copy-start = (f32[1,4,8,8,1024]{4,3,2,1,0:T(8,128)S(1)}, f32[1,4,8,8,1024]{4,3,2,1,0:T(8,128)}, u32[]{:S(2)}) copy-start(f32[1,4,8,8,1024]{4,3,2,1,0:T(8,128)} %param.13) | copy-start | bytes 3145732
  38.4 363.7 %reduce-scatter.2.cloned.1.call-start = ((), (), s32[]{:S(2)}) async-start(), calls=%async_computation.2 | async-start | bytes 1572864 | tf_op jit(solution)/shard_map/reduce_scatter | solution.py:135
  39.2 28.9 %collective-permute-start.2 = (f32[4,8,1,1024]{3,2,1,0:T(1,128)}, f32[4,8,1,1024]{3,2,1,0:T(1,128)}, u32[]{:S(2)}, u32[]{:S(2)}) collective-permute-start(f32[4,8,1,1024]{3,2,1,0:T(1,128)} %get-tuple-element.83), channel_id=1, source_target_pairs={{1,0},{2,1},{3,2},{4,3},{5,4},{6,5},{7,6},{9,8},{10,9},{11,10},{12... | collective-permute-start | bytes 393224 | tf_op jit(solution)/shard_map/ppermute | solution.py:16
  41.2 28.3 %collective-permute-start.3 = (f32[4,8,1,1024]{3,2,1,0:T(1,128)S(1)}, f32[4,8,1,1024]{3,2,1,0:T(1,128)}, u32[]{:S(2)}, u32[]{:S(2)}) collective-permute-start(f32[4,8,1,1024]{3,2,1,0:T(1,128)S(1)} %get-tuple-element.82), channel_id=1, source_target_pairs={{0,1},{1,2},{2,3},{3,4},{4,5},{5,6},{6,7},{8,9},{9,10},{10,11},{11... | collective-permute-start | bytes 393224 | tf_op jit(solution)/shard_map/ppermute | solution.py:15
  62.0 2.3 copy-start.43
  64.9 3.2 copy-start.39
  64.9 4.5 %copy-start.38 = (f32[4,1,8,1024]{3,2,1,0:T(8,128)S(1)}, f32[4,1,8,1024]{3,2,1,0:T(8,128)}, u32[]{:S(2)}) copy-start(f32[4,1,8,1024]{3,2,1,0:T(8,128)} %get-tuple-element.78) | copy-start | bytes 393220
  64.9 9.2 %copy-start.13 = (f32[4,8,7,1024]{3,2,1,0:T(8,128)S(1)}, f32[4,8,7,1024]{3,2,1,0:T(8,128)}, u32[]{:S(2)}) copy-start(f32[4,8,7,1024]{3,2,1,0:T(8,128)} %get-tuple-element.85) | copy-start | bytes 2752516
  68.1 8.6 %collective-permute-start = (f32[4,1,8,1024]{3,2,1,0:T(8,128)S(1)}, f32[4,1,8,1024]{3,2,1,0:T(8,128)S(1)}, u32[]{:S(2)}, u32[]{:S(2)}) collective-permute-start(f32[4,1,8,1024]{3,2,1,0:T(8,128)S(1)} %copy-done.39), channel_id=1, source_target_pairs={{8,0},{16,8},{24,16},{32,24},{40,32},{48,40},{56,48},{9,1},{17,9},... | collective-permute-start | bytes 393224 | tf_op jit(solution)/shard_map/ppermute | solution.py:16
  69.4 10.0 %collective-permute-start.1 = (f32[4,1,8,1024]{3,2,1,0:T(8,128)S(1)}, f32[4,1,8,1024]{3,2,1,0:T(8,128)S(1)}, u32[]{:S(2)}, u32[]{:S(2)}) collective-permute-start(f32[4,1,8,1024]{3,2,1,0:T(8,128)S(1)} %copy-done.38), channel_id=1, source_target_pairs={{0,8},{8,16},{16,24},{24,32},{32,40},{40,48},{48,56},{1,9},{9,17},... | collective-permute-start | bytes 393224 | tf_op jit(solution)/shard_map/ppermute | solution.py:15
  74.2 2.6 copy-start.37
  74.2 5.3 %copy-start.30 = (f32[4,7,8,1024]{3,2,1,0:T(8,128)S(1)}, f32[4,7,8,1024]{3,2,1,0:T(8,128)}, u32[]{:S(2)}) copy-start(f32[4,7,8,1024]{3,2,1,0:T(8,128)} %get-tuple-element.80) | copy-start | bytes 2752516
  74.2 5.3 %copy-start.31 = (f32[4,7,8,1024]{3,2,1,0:T(8,128)S(1)}, f32[4,7,8,1024]{3,2,1,0:T(8,128)}, u32[]{:S(2)}) copy-start(f32[4,7,8,1024]{3,2,1,0:T(8,128)} %get-tuple-element.81) | copy-start | bytes 2752516
  76.8 8.8 %collective-permute-start.7 = (bf16[4,4,8,1,1024]{4,3,2,1,0:T(2,128)(2,1)S(1)}, bf16[4,4,8,1,1024]{4,3,2,1,0:T(2,128)(2,1)S(1)}, u32[]{:S(2)}, u32[]{:S(2)}) collective-permute-start(bf16[4,4,8,1,1024]{4,3,2,1,0:T(2,128)(2,1)S(1)} %copy-done.37), channel_id=1, source_target_pairs={{0,1},{1,2},{2,3},{3,4},{4,5},{5,6},{6,7},{8,9},{9,10},{10,11},{11... | collective-permute-start | bytes 786440 | tf_op jit(solution)/shard_map/ppermute | solution.py:15
  79.5 2.4 copy-start.29
  83.2 2.9 copy-start.18
  83.2 2.9 copy-start.19
  87.7 1.9 copy-start.17
  96.0 138.6 %copy-start.44 = (f32[256,1]{0,1:T(1,128)S(1)}, f32[256,1]{0,1:T(1,128)}, u32[]{:S(2)}) copy-start(f32[256,1]{0,1:T(1,128)} %get-tuple-element.146) | copy-start | bytes 3076
  96.0 138.6 %copy-start.45 = (f32[256,1]{0,1:T(1,128)S(1)}, f32[256,1]{0,1:T(1,128)}, u32[]{:S(2)}) copy-start(f32[256,1]{0,1:T(1,128)} %get-tuple-element.147) | copy-start | bytes 3076
  96.0 138.6 %copy-start.46 = (f32[256,1]{0,1:T(1,128)S(1)}, f32[256,1]{0,1:T(1,128)}, u32[]{:S(2)}) copy-start(f32[256,1]{0,1:T(1,128)} %get-tuple-element.148) | copy-start | bytes 3076
  96.0 138.6 %copy-start.47 = (pred[256]{0:T(512)(128)(4,1)S(1)}, pred[256]{0:T(512)(128)(4,1)}, u32[]{:S(2)}) copy-start(pred[256]{0:T(512)(128)(4,1)} %get-tuple-element.164) | copy-start | bytes 772
  243.2 25.4 %collective-permute-start.10 = (f32[8,1,1024]{2,1,0:T(1,128)}, f32[8,1,1024]{2,1,0:T(1,128)}, u32[]{:S(2)}, u32[]{:S(2)}) collective-permute-start(f32[8,1,1024]{2,1,0:T(1,128)} %get-tuple-element.135), channel_id=1, source_target_pairs={{1,0},{2,1},{3,2},{4,3},{5,4},{6,5},{7,6},{9,8},{10,9},{11,10},{12... | collective-permute-start | bytes 98312 | tf_op jit(solution)/shard_map/ppermute | solution.py:16
  246.3 22.3 %collective-permute-start.11 = (f32[8,1,1024]{2,1,0:T(1,128)}, f32[8,1,1024]{2,1,0:T(1,128)}, u32[]{:S(2)}, u32[]{:S(2)}) collective-permute-start(f32[8,1,1024]{2,1,0:T(1,128)} %get-tuple-element.134), channel_id=1, source_target_pairs={{0,1},{1,2},{2,3},{3,4},{4,5},{5,6},{6,7},{8,9},{9,10},{10,11},{11... | collective-permute-start | bytes 98312 | tf_op jit(solution)/shard_map/ppermute | solution.py:15
  249.7 20.2 %collective-permute-start.8 = (f32[1,8,1024]{2,1,0:T(8,128)S(1)}, f32[1,8,1024]{2,1,0:T(8,128)S(1)}, u32[]{:S(2)}, u32[]{:S(2)}) collective-permute-start(f32[1,8,1024]{2,1,0:T(8,128)S(1)} %get-tuple-element.131), channel_id=1, source_target_pairs={{8,0},{16,8},{24,16},{32,24},{40,32},{48,40},{56,48},{9,1},{17,9},... | collective-permute-start | bytes 98312 | tf_op jit(solution)/shard_map/ppermute | solution.py:16
  251.0 18.9 %collective-permute-start.9 = (f32[1,8,1024]{2,1,0:T(8,128)S(1)}, f32[1,8,1024]{2,1,0:T(8,128)S(1)}, u32[]{:S(2)}, u32[]{:S(2)}) collective-permute-start(f32[1,8,1024]{2,1,0:T(8,128)S(1)} %get-tuple-element.130), channel_id=1, source_target_pairs={{0,8},{8,16},{16,24},{24,32},{32,40},{40,48},{48,56},{1,9},{9,17},... | collective-permute-start | bytes 98312 | tf_op jit(solution)/shard_map/ppermute | solution.py:15
  268.6 2.4 copy-start.11
  268.6 2.4 copy-start.36
  271.0 2.0 copy-start.2
  271.0 2.0 copy-start.8
  275.1 11.6 %collective-permute-start.14 = (f32[4,8,1,1024]{3,2,1,0:T(1,128)S(1)}, f32[4,8,1,1024]{3,2,1,0:T(1,128)S(1)}, u32[]{:S(2)}, u32[]{:S(2)}) collective-permute-start(f32[4,8,1,1024]{3,2,1,0:T(1,128)S(1)} %get-tuple-element.69), channel_id=1, source_target_pairs={{1,0},{2,1},{3,2},{4,3},{5,4},{6,5},{7,6},{9,8},{10,9},{11,10},{12... | collective-permute-start | bytes 393224 | tf_op jit(solution)/shard_map/ppermute | solution.py:16
  278.3 8.3 %collective-permute-start.15 = (f32[4,8,1,1024]{3,2,1,0:T(1,128)S(1)}, f32[4,8,1,1024]{3,2,1,0:T(1,128)S(1)}, u32[]{:S(2)}, u32[]{:S(2)}) collective-permute-start(f32[4,8,1,1024]{3,2,1,0:T(1,128)S(1)} %get-tuple-element.68), channel_id=1, source_target_pairs={{0,1},{1,2},{2,3},{3,4},{4,5},{5,6},{6,7},{8,9},{9,10},{10,11},{11... | collective-permute-start | bytes 393224 | tf_op jit(solution)/shard_map/ppermute | solution.py:15
  280.6 7.1 %collective-permute-start.12 = (f32[4,1,8,1024]{3,2,1,0:T(8,128)S(1)}, f32[4,1,8,1024]{3,2,1,0:T(8,128)S(1)}, u32[]{:S(2)}, u32[]{:S(2)}) collective-permute-start(f32[4,1,8,1024]{3,2,1,0:T(8,128)S(1)} %get-tuple-element.65), channel_id=1, source_target_pairs={{8,0},{16,8},{24,16},{32,24},{40,32},{48,40},{56,48},{9,1},{17,9},... | collective-permute-start | bytes 393224 | tf_op jit(solution)/shard_map/ppermute | solution.py:16
  281.9 6.7 %collective-permute-start.13 = (f32[4,1,8,1024]{3,2,1,0:T(8,128)S(1)}, f32[4,1,8,1024]{3,2,1,0:T(8,128)S(1)}, u32[]{:S(2)}, u32[]{:S(2)}) collective-permute-start(f32[4,1,8,1024]{3,2,1,0:T(8,128)S(1)} %get-tuple-element.64), channel_id=1, source_target_pairs={{0,8},{8,16},{16,24},{24,32},{32,40},{40,48},{48,56},{1,9},{9,17},... | collective-permute-start | bytes 393224 | tf_op jit(solution)/shard_map/ppermute | solution.py:15
  286.7 2.2 copy-start.12
  286.7 2.2 copy-start.35
  288.6 1.9 copy-start.9
  290.9 12.6 %collective-permute-start.18 = (f32[8,1,1024]{2,1,0:T(1,128)S(1)}, f32[8,1,1024]{2,1,0:T(1,128)S(1)}, u32[]{:S(2)}, u32[]{:S(2)}) collective-permute-start(f32[8,1,1024]{2,1,0:T(1,128)S(1)} %get-tuple-element.127), channel_id=1, source_target_pairs={{1,0},{2,1},{3,2},{4,3},{5,4},{6,5},{7,6},{9,8},{10,9},{11,10},{12... | collective-permute-start | bytes 98312 | tf_op jit(solution)/shard_map/ppermute | solution.py:16
  293.9 9.6 %collective-permute-start.19 = (f32[8,1,1024]{2,1,0:T(1,128)S(1)}, f32[8,1,1024]{2,1,0:T(1,128)S(1)}, u32[]{:S(2)}, u32[]{:S(2)}) collective-permute-start(f32[8,1,1024]{2,1,0:T(1,128)S(1)} %get-tuple-element.126), channel_id=1, source_target_pairs={{0,1},{1,2},{2,3},{3,4},{4,5},{5,6},{6,7},{8,9},{9,10},{10,11},{11... | collective-permute-start | bytes 98312 | tf_op jit(solution)/shard_map/ppermute | solution.py:15
  296.7 6.9 %collective-permute-start.16 = (f32[1,8,1024]{2,1,0:T(8,128)S(1)}, f32[1,8,1024]{2,1,0:T(8,128)S(1)}, u32[]{:S(2)}, u32[]{:S(2)}) collective-permute-start(f32[1,8,1024]{2,1,0:T(8,128)S(1)} %get-tuple-element.123), channel_id=1, source_target_pairs={{8,0},{16,8},{24,16},{32,24},{40,32},{48,40},{56,48},{9,1},{17,9},... | collective-permute-start | bytes 98312 | tf_op jit(solution)/shard_map/ppermute | solution.py:16
  298.0 6.5 %collective-permute-start.17 = (f32[1,8,1024]{2,1,0:T(8,128)S(1)}, f32[1,8,1024]{2,1,0:T(8,128)S(1)}, u32[]{:S(2)}, u32[]{:S(2)}) collective-permute-start(f32[1,8,1024]{2,1,0:T(8,128)S(1)} %get-tuple-element.122), channel_id=1, source_target_pairs={{0,8},{8,16},{16,24},{24,32},{32,40},{40,48},{48,56},{1,9},{9,17},... | collective-permute-start | bytes 98312 | tf_op jit(solution)/shard_map/ppermute | solution.py:15
  306.3 12.9 %collective-permute-start.22 = (f32[4,8,1,1024]{3,2,1,0:T(1,128)S(1)}, f32[4,8,1,1024]{3,2,1,0:T(1,128)S(1)}, u32[]{:S(2)}, u32[]{:S(2)}) collective-permute-start(f32[4,8,1,1024]{3,2,1,0:T(1,128)S(1)} %get-tuple-element.55), channel_id=1, source_target_pairs={{1,0},{2,1},{3,2},{4,3},{5,4},{6,5},{7,6},{9,8},{10,9},{11,10},{12... | collective-permute-start | bytes 393224 | tf_op jit(solution)/shard_map/ppermute | solution.py:16
  308.2 11.0 %collective-permute-start.23 = (f32[4,8,1,1024]{3,2,1,0:T(1,128)S(1)}, f32[4,8,1,1024]{3,2,1,0:T(1,128)S(1)}, u32[]{:S(2)}, u32[]{:S(2)}) collective-permute-start(f32[4,8,1,1024]{3,2,1,0:T(1,128)S(1)} %get-tuple-element.54), channel_id=1, source_target_pairs={{0,1},{1,2},{2,3},{3,4},{4,5},{5,6},{6,7},{8,9},{9,10},{10,11},{11... | collective-permute-start | bytes 393224 | tf_op jit(solution)/shard_map/ppermute | solution.py:15
  311.8 7.8 %collective-permute-start.20 = (f32[4,1,8,1024]{3,2,1,0:T(8,128)S(1)}, f32[4,1,8,1024]{3,2,1,0:T(8,128)S(1)}, u32[]{:S(2)}, u32[]{:S(2)}) collective-permute-start(f32[4,1,8,1024]{3,2,1,0:T(8,128)S(1)} %get-tuple-element.51), channel_id=1, source_target_pairs={{8,0},{16,8},{24,16},{32,24},{40,32},{48,40},{56,48},{9,1},{17,9},... | collective-permute-start | bytes 393224 | tf_op jit(solution)/shard_map/ppermute | solution.py:16
  313.1 8.0 %collective-permute-start.21 = (f32[4,1,8,1024]{3,2,1,0:T(8,128)S(1)}, f32[4,1,8,1024]{3,2,1,0:T(8,128)S(1)}, u32[]{:S(2)}, u32[]{:S(2)}) collective-permute-start(f32[4,1,8,1024]{3,2,1,0:T(8,128)S(1)} %get-tuple-element.50), channel_id=1, source_target_pairs={{0,8},{8,16},{16,24},{24,32},{32,40},{40,48},{48,56},{1,9},{9,17},... | collective-permute-start | bytes 393224 | tf_op jit(solution)/shard_map/ppermute | solution.py:15
  323.1 12.6 %collective-permute-start.26 = (f32[8,1,1024]{2,1,0:T(1,128)S(1)}, f32[8,1,1024]{2,1,0:T(1,128)S(1)}, u32[]{:S(2)}, u32[]{:S(2)}) collective-permute-start(f32[8,1,1024]{2,1,0:T(1,128)S(1)} %get-tuple-element.119), channel_id=1, source_target_pairs={{1,0},{2,1},{3,2},{4,3},{5,4},{6,5},{7,6},{9,8},{10,9},{11,10},{12... | collective-permute-start | bytes 98312 | tf_op jit(solution)/shard_map/ppermute | solution.py:16
  325.1 10.6 %collective-permute-start.27 = (f32[8,1,1024]{2,1,0:T(1,128)S(1)}, f32[8,1,1024]{2,1,0:T(1,128)S(1)}, u32[]{:S(2)}, u32[]{:S(2)}) collective-permute-start(f32[8,1,1024]{2,1,0:T(1,128)S(1)} %get-tuple-element.118), channel_id=1, source_target_pairs={{0,1},{1,2},{2,3},{3,4},{4,5},{5,6},{6,7},{8,9},{9,10},{10,11},{11... | collective-permute-start | bytes 98312 | tf_op jit(solution)/shard_map/ppermute | solution.py:15
  328.9 6.9 %collective-permute-start.24 = (f32[1,8,1024]{2,1,0:T(8,128)S(1)}, f32[1,8,1024]{2,1,0:T(8,128)S(1)}, u32[]{:S(2)}, u32[]{:S(2)}) collective-permute-start(f32[1,8,1024]{2,1,0:T(8,128)S(1)} %get-tuple-element.115), channel_id=1, source_target_pairs={{8,0},{16,8},{24,16},{32,24},{40,32},{48,40},{56,48},{9,1},{17,9},... | collective-permute-start | bytes 98312 | tf_op jit(solution)/shard_map/ppermute | solution.py:16
  330.2 6.5 %collective-permute-start.25 = (f32[1,8,1024]{2,1,0:T(8,128)S(1)}, f32[1,8,1024]{2,1,0:T(8,128)S(1)}, u32[]{:S(2)}, u32[]{:S(2)}) collective-permute-start(f32[1,8,1024]{2,1,0:T(8,128)S(1)} %get-tuple-element.114), channel_id=1, source_target_pairs={{0,8},{8,16},{16,24},{24,32},{32,40},{40,48},{48,56},{1,9},{9,17},... | collective-permute-start | bytes 98312 | tf_op jit(solution)/shard_map/ppermute | solution.py:15
  338.4 12.8 %collective-permute-start.30 = (f32[4,8,1,1024]{3,2,1,0:T(1,128)S(1)}, f32[4,8,1,1024]{3,2,1,0:T(1,128)S(1)}, u32[]{:S(2)}, u32[]{:S(2)}) collective-permute-start(f32[4,8,1,1024]{3,2,1,0:T(1,128)S(1)} %get-tuple-element.41), channel_id=1, source_target_pairs={{1,0},{2,1},{3,2},{4,3},{5,4},{6,5},{7,6},{9,8},{10,9},{11,10},{12... | collective-permute-start | bytes 393224 | tf_op jit(solution)/shard_map/ppermute | solution.py:16
  340.3 10.9 %collective-permute-start.31 = (f32[4,8,1,1024]{3,2,1,0:T(1,128)S(1)}, f32[4,8,1,1024]{3,2,1,0:T(1,128)S(1)}, u32[]{:S(2)}, u32[]{:S(2)}) collective-permute-start(f32[4,8,1,1024]{3,2,1,0:T(1,128)S(1)} %get-tuple-element.40), channel_id=1, source_target_pairs={{0,1},{1,2},{2,3},{3,4},{4,5},{5,6},{6,7},{8,9},{9,10},{10,11},{11... | collective-permute-start | bytes 393224 | tf_op jit(solution)/shard_map/ppermute | solution.py:15
  344.0 7.7 %collective-permute-start.28 = (f32[4,1,8,1024]{3,2,1,0:T(8,128)S(1)}, f32[4,1,8,1024]{3,2,1,0:T(8,128)S(1)}, u32[]{:S(2)}, u32[]{:S(2)}) collective-permute-start(f32[4,1,8,1024]{3,2,1,0:T(8,128)S(1)} %get-tuple-element.37), channel_id=1, source_target_pairs={{8,0},{16,8},{24,16},{32,24},{40,32},{48,40},{56,48},{9,1},{17,9},... | collective-permute-start | bytes 393224 | tf_op jit(solution)/shard_map/ppermute | solution.py:16
  345.3 7.9 %collective-permute-start.29 = (f32[4,1,8,1024]{3,2,1,0:T(8,128)S(1)}, f32[4,1,8,1024]{3,2,1,0:T(8,128)S(1)}, u32[]{:S(2)}, u32[]{:S(2)}) collective-permute-start(f32[4,1,8,1024]{3,2,1,0:T(8,128)S(1)} %get-tuple-element.36), channel_id=1, source_target_pairs={{0,8},{8,16},{16,24},{24,32},{32,40},{40,48},{48,56},{1,9},{9,17},... | collective-permute-start | bytes 393224 | tf_op jit(solution)/shard_map/ppermute | solution.py:15
  355.2 12.5 %collective-permute-start.34 = (f32[8,1,1024]{2,1,0:T(1,128)S(1)}, f32[8,1,1024]{2,1,0:T(1,128)S(1)}, u32[]{:S(2)}, u32[]{:S(2)}) collective-permute-start(f32[8,1,1024]{2,1,0:T(1,128)S(1)} %get-tuple-element.103), channel_id=1, source_target_pairs={{1,0},{2,1},{3,2},{4,3},{5,4},{6,5},{7,6},{9,8},{10,9},{11,10},{12... | collective-permute-start | bytes 98312 | tf_op jit(solution)/shard_map/ppermute | solution.py:16
  357.1 10.5 %collective-permute-start.35 = (f32[8,1,1024]{2,1,0:T(1,128)S(1)}, f32[8,1,1024]{2,1,0:T(1,128)S(1)}, u32[]{:S(2)}, u32[]{:S(2)}) collective-permute-start(f32[8,1,1024]{2,1,0:T(1,128)S(1)} %get-tuple-element.102), channel_id=1, source_target_pairs={{0,1},{1,2},{2,3},{3,4},{4,5},{5,6},{6,7},{8,9},{9,10},{10,11},{11... | collective-permute-start | bytes 98312 | tf_op jit(solution)/shard_map/ppermute | solution.py:15
  361.0 6.8 %collective-permute-start.32 = (f32[1,8,1024]{2,1,0:T(8,128)S(1)}, f32[1,8,1024]{2,1,0:T(8,128)S(1)}, u32[]{:S(2)}, u32[]{:S(2)}) collective-permute-start(f32[1,8,1024]{2,1,0:T(8,128)S(1)} %get-tuple-element.99), channel_id=1, source_target_pairs={{8,0},{16,8},{24,16},{32,24},{40,32},{48,40},{56,48},{9,1},{17,9},... | collective-permute-start | bytes 98312 | tf_op jit(solution)/shard_map/ppermute | solution.py:16
  362.3 6.4 %collective-permute-start.33 = (f32[1,8,1024]{2,1,0:T(8,128)S(1)}, f32[1,8,1024]{2,1,0:T(8,128)S(1)}, u32[]{:S(2)}, u32[]{:S(2)}) collective-permute-start(f32[1,8,1024]{2,1,0:T(8,128)S(1)} %get-tuple-element.98), channel_id=1, source_target_pairs={{0,8},{8,16},{16,24},{24,32},{32,40},{40,48},{48,56},{1,9},{9,17},... | collective-permute-start | bytes 98312 | tf_op jit(solution)/shard_map/ppermute | solution.py:15
  (23 other events, 31.8 us)
Sparse Core Ops, SparseCore 0:
  38.5 194.5 all-gather.1
  371.9 30.0 reduce-scatter.1
